TPU v7x, 256 devices: a whole 4x4x8 slice. The times are simulated.
256 devices in a mesh: dp: 32 (over z, x_lo, core), tp: 8 (over x_hi, y).
Axes of the slice: x: 4 (x_hi: 2, x_lo: 2; x = x_hi * 2 + x_lo), y: 4, z: 8, core: 2. Of those that a mesh axis runs over, the one named last changes fastest.
Arguments:
- queries: bfloat16 [256, 8192], P('dp', 'tp'), may hold values from -5 to 5
- prefix_kv: bfloat16 [2, 65536, 1024], P(None, 'dp', 'tp'), may hold values from -5 to 5
- cache_kv: bfloat16 [2, 2048, 64, 1024], P(None, 'dp', None, 'tp'), may hold values from -5 to 5
- lengths: int32 [256], P('dp'), may hold values from 1 to 512, as said below
- page_table: int32 [32, 64], P('dp'), may hold values from 0 to 63, each once within a row
- owner: int32 [32], replicated, may hold values from 0 to 31, as said below
- readers: int32 [16], replicated, may hold values from 0 to 31, as said below
- w_out: bfloat16 [8192, 4096], P('tp'), may hold values from -0.5 to 0.5
Outputs:
- projected: bfloat16 [256, 4096], P('dp', 'tp')
Inputs may be any that keep to these rules, and one draw needn't show every extreme that they name: `lengths`: at most 512, reached by some request in every draw. `page_table`: each row holds every page id of its replica once. `owner`: every replica index once. `readers`: 16 distinct replica indices, none of them owner[0].
All inputs are finite; a program needn't handle non-finite values.
Results may differ from a plain program's by a relative error of at most 0.0051.
Values may be sent and summed in bfloat16 or wider, within the bound.
A program may use at most 64 MiB of HBM per device.

v0:
```python
import jax
import jax.numpy as jnp
from jax import lax
from jax.sharding import PartitionSpec as P

HD = 128
PREFIX = 2048
PAGE = 64


def padded_to(lines, length):
    spare = -lines.shape[0] % length
    if not spare:
        return lines
    return jnp.concatenate([lines, jnp.zeros((spare, *lines.shape[1:]), lines.dtype)])


def broadcast_by_parts(value, axis, root):
    lines = jnp.where(lax.axis_index(axis) == root, value, jnp.zeros_like(value)).reshape(
        -1, *value.shape[1:][-1:]
    )
    padded = padded_to(lines, lax.axis_size(axis))
    own = lax.psum_scatter(padded, axis, scatter_dimension=0, tiled=True)
    return lax.all_gather(own, axis, axis=0, tiled=True)[: len(lines)].reshape(value.shape)


def cut_along(value, dim, length):
    lengths = value.shape
    tiles = value.reshape(*lengths[:dim], length, lengths[dim] // length, *lengths[dim + 1 :])
    return jnp.moveaxis(tiles, dim, 0)


def sum_at_owner(value, axis, dim):
    length = lax.axis_size(axis)
    tiles = lax.all_to_all(cut_along(value, dim, length), axis, 0, 0, tiled=True)
    return jnp.sum(tiles, axis=0)


def shards(queries, prefix_kv, cache_kv, lengths, page_table, owner, readers, w_out):
    rows = queries.shape[0]
    heads_here = queries.shape[1] // HD
    groups_here = prefix_kv.shape[2] // HD
    group = heads_here // groups_here
    maxpages = page_table.shape[1] // rows
    scale = 1.0 / HD**0.5
    replica_id = lax.axis_index("dp")
    matches = readers == replica_id
    is_reader = jnp.any(matches)
    query = queries.reshape(rows, groups_here, group, HD)
    pages = page_table[0].reshape(rows, maxpages)
    resident = cache_kv[:, pages].reshape(2, rows, maxpages * PAGE, groups_here, HD)
    s_res = (
        jnp.einsum("bkgd,btkd->bkgt", query, resident[0], preferred_element_type=jnp.float32)
        * scale
    )
    inside = jnp.arange(maxpages * PAGE, dtype=jnp.int32)[None, :] < lengths[:, None]
    s_res = jnp.where(inside[:, None, None, :], s_res, -jnp.inf)
    top_res = jnp.max(s_res, axis=-1)
    shared = broadcast_by_parts(prefix_kv, "dp", owner[0])
    shared = shared.reshape(2, PREFIX, groups_here, HD)
    s_pre = (
        jnp.einsum("bkgd,tkd->bkgt", query, shared[0], preferred_element_type=jnp.float32) * scale
    )
    s_pre = jnp.where(is_reader, s_pre, -jnp.inf)
    top = jnp.maximum(top_res, jnp.max(s_pre, axis=-1))
    e_pre = jnp.exp(s_pre - top[..., None])
    den_pre = jnp.sum(e_pre, axis=-1)
    num_pre = jnp.einsum(
        "bkgt,tkd->bkgd", e_pre.astype(jnp.bfloat16), shared[1], preferred_element_type=jnp.float32
    )
    e_res = jnp.exp(s_res - top[..., None])
    den = jnp.sum(e_res, axis=-1) + den_pre
    num = (
        jnp.einsum(
            "bkgt,btkd->bkgd",
            e_res.astype(jnp.bfloat16),
            resident[1],
            preferred_element_type=jnp.float32,
        )
        + num_pre
    )
    attn = (num / den[..., None]).astype(jnp.bfloat16).reshape(rows, heads_here * HD)
    partial_out = jnp.dot(attn, w_out, preferred_element_type=jnp.float32)
    return sum_at_owner(partial_out, "tp", 1).astype(jnp.bfloat16)


def solution(mesh):
    placed = (
        P("dp", "tp"),
        P(None, "dp", "tp"),
        P(None, "dp", None, "tp"),
        P("dp"),
        P("dp", None),
        P(),
        P(),
        P("tp", None),
    )
    return jax.shard_map(
        shards, mesh=mesh, in_specs=placed, out_specs=P("dp", "tp"), check_vma=False
    )
```

profile of v0, /device:TPU:1, one launch (start us, length us, event | category | flops | bytes accessed | tf_op | source)
XLA Modules:
  0.0 223.7 jit_solution(934141285971091137)
XLA Ops:
  6.5 0.0 copy-start
  6.5 0.0 reduce-scatter.2.cloned.1.call-start
  7.4 1.1 broadcast_select_fusion
  8.4 0.0 reduce-scatter.2.cloned.1.call-update
  8.5 0.0 all-gather.2.cloned.1.call-start
  8.5 118.1 %reduce-scatter.2.cloned.1.call-done = bf16[128,128]{1,0:T(8,128)(2,1)} async-done(((bf16[4096,128]{1,0:T(8,128)(2,1)}), bf16[128,128]{1,0:T(8,128)(2,1)}) %reduce-scatter.2.cloned.1.call-update) | async-done | bytes 32784 | tf_op jit(solution)/shard_map/reduce_scatter | solution.py:23
  126.6 0.0 all-gather.2.cloned.1.call-update
  126.6 0.5 broadcast.55
  127.1 0.0 copy-done.4
  127.1 0.7 reduce.9
  127.8 0.1 reshape_squeeze.3
  127.9 0.1 reshape.140
  128.0 0.0 copy-done
  128.0 2.2 gather_fusion
  130.2 3.2 %copy.23 = bf16[8,8,2,64,128]{4,3,1,0,2:T(8,128)(2,1)} copy(bf16[8,8,2,64,128]{4,3,2,1,0:T(8,128)(2,1)} %bitcast.54) | data formatting | bytes 4194304 | tf_op jit(solution)/shard_map/gather | solution.py:51
  133.4 12.0 %copy.13 = bf16[4096,1024]{1,0:T(8,128)(2,1)} copy(bf16[4096,1024]{0,1:T(8,128)(2,1)} %bitcast.55) | data formatting | bytes 16777216 | tf_op jit(solution)/shard_map/dot_general | solution.py:83
  145.4 0.0 copy-done.5
  145.4 0.6 compare_reduce_fusion
  146.0 0.0 copy-done.2
  146.0 0.1 iota_compare_fusion
  146.1 1.8 fusion.18
  147.9 0.0 copy-done.1
  147.9 0.5 fusion.19
  148.4 46.1 %all-gather.2.cloned.1.call-done = bf16[4096,128]{1,0:T(8,128)(2,1)} async-done(((bf16[128,128]{1,0:T(8,128)(2,1)}), bf16[4096,128]{1,0:T(8,128)(2,1)}) %all-gather.2.cloned.1.call-update) | async-done | bytes 1048592 | tf_op jit(solution)/shard_map/all_gather | solution.py:24
  194.5 2.1 fusion.20
  196.7 0.2 fusion.12
  196.8 0.3 convolution_bitcast_fusion.2
  197.1 0.2 fusion.7
  197.4 0.3 fusion.6
  197.7 5.6 %convolution_bitcast_fusion = f32[8,8,512]{2,1,0:T(8,128)S(1)} fusion(bf16[8,1024,1]{1,0,2:T(8,128)(2,1)S(1)} %reshape.149, bf16[8,512,1024]{2,1,0:T(8,128)(2,1)} %bitcast.53), kind=kOutput, calls=%fused_computation.5 | convolution fusion | flops 67108864 | bytes 8536064 | tf_op jit(solution)/shard_map/dot_general | solution.py:83
  203.3 12.9 %all_to_all.5 = f32[8,8,512]{2,1,0:T(8,128)S(1)} all-to-all(f32[8,8,512]{2,1,0:T(8,128)S(1)} %convolution_bitcast_fusion), channel_id=1, replica_groups=mesh['dp'=32,'tp'=8] {'tp'}, dimensions={0} | all-to-all | bytes 262144 | tf_op jit(solution)/shard_map/all_to_all | solution.py:35
  216.2 0.6 reduce_sum.29
  (11 shorter events, 0.1 us)
Async XLA Ops:
  6.5 121.5 %copy-start = (bf16[2,64,64,128]{3,2,1,0:T(8,128)(2,1)S(1)}, bf16[2,64,64,128]{3,2,1,0:T(8,128)(2,1)}, u32[]{:S(2)}) copy-start(bf16[2,64,64,128]{3,2,1,0:T(8,128)(2,1)} %param.10) | copy-start | bytes 6291460
  6.5 120.6 %copy-start.4 = (s32[1,64]{1,0:T(1,128)S(1)}, s32[1,64]{1,0:T(1,128)}, u32[]{:S(2)}) copy-start(s32[1,64]{1,0:T(1,128)} %param.12) | copy-start | bytes 772
  6.5 120.1 %reduce-scatter.2.cloned.1.call-start = ((), (), s32[]{:S(2)}) async-start(), calls=%async_computation.2 | async-start | bytes 1081344 | tf_op jit(solution)/shard_map/reduce_scatter | solution.py:23
  8.5 186.0 %all-gather.2.cloned.1.call-start = ((), (), s32[]{:S(2)}) async-start(), calls=%async_computation.3 | async-start | bytes 1081344 | tf_op jit(solution)/shard_map/all_gather | solution.py:24
  133.4 12.0 %copy-start.5 = (s32[16]{0:T(128)S(1)}, s32[16]{0:T(128)}, u32[]{:S(2)}) copy-start(s32[16]{0:T(128)} %param.14) | copy-start | bytes 196
  133.4 12.7 %copy-start.2 = (s32[8]{0:T(128)S(1)}, s32[8]{0:T(128)}, u32[]{:S(2)}) copy-start(s32[8]{0:T(128)} %param.11) | copy-start | bytes 100
  146.1 1.8 copy-start.1
  194.5 2.9 %copy-start.3 = (bf16[4096,128]{1,0:T(8,128)(2,1)S(1)}, bf16[4096,128]{1,0:T(8,128)(2,1)}, u32[]{:S(2)}) copy-start(bf16[4096,128]{1,0:T(8,128)(2,1)} %all-gather.2.cloned.1.call-done) | copy-start | bytes 3145732
Sparse Core Ops, SparseCore 0:
  9.9 116.7 reduce-scatter.1
  128.6 65.8 all-gather.1
where the time goes:
time: 224 us
  waiting for transfers between devices  164 us (73%)
  local copies, waits for them, and re-layouts  19.9 us (9%)
  between operations  14.3 us (6%)
  blocking collectives  12.9 us (6%)
  matrix products  8.83 us (4%)
  other arithmetic  3.49 us (2%)
    reduce_scatter x1, waiting for transfers between devices, broadcast_by_parts(): own = lax.psum_scatter(padded, axis, scatter_dimension=0, tiled=True)  118 us
    all_gather x1, waiting for transfers between devices, broadcast_by_parts(): lax.all_gather(own, axis, axis=0, tiled=True)[:len(lines)]  46.1 us
    all_to_all x1, blocking collectives, sum_at_owner(): lax.all_to_all(cut_along(value, dim, length), axis, 0, 0, tiled=True)  12.9 us
    dot_general x1, local copies, waits for them, and re-layouts, shards(): partial_out = jnp.dot(attn, w_out, preferred_element_type=jnp.float32)  12 us
    dot_general x1, matrix products, shards(): partial_out = jnp.dot(attn, w_out, preferred_element_type=jnp.float32)  5.64 us
    gather x2, local copies, waits for them, and re-layouts, shards(): cache_kv[:, pages].reshape(2, rows, maxpages * PAGE, groups_here, HD)  5.39 us
  transfers between devices with their start and end apart: 2, of which 2 were waited for; matrix products, arithmetic and copies ran while one was open for 10% of the time, Pallas kernels for 0%

commit v1 on v0

--- a/solution.py
+++ b/solution.py
@@ -21,7 +21,9 @@
     )
     padded = padded_to(lines, lax.axis_size(axis))
     own = lax.psum_scatter(padded, axis, scatter_dimension=0, tiled=True)
-    return lax.all_gather(own, axis, axis=0, tiled=True)[: len(lines)].reshape(value.shape)
+    return jnp.concatenate(
+        lax.all_to_all(jnp.stack([own] * lax.axis_size(axis)), axis, 0, 0), axis=0
+    )[: len(lines)].reshape(value.shape)
 
 
 def cut_along(value, dim, length):

time: 224 us -> 195 us (0.87)
  waiting for transfers between devices: 164 us -> 124 us
  starting transfers between devices: 0.04 us -> 8.78 us
  local copies, waits for them, and re-layouts: 19.9 us -> 22.8 us
    all_gather x1 -> x0, waiting for transfers between devices: 46.1 us -> none  [broadcast_by_parts(): lax.all_gather(own, axis, axis=0, tiled=True)[:len(lines)]]
    all_to_all x0 -> x1, starting transfers between devices: none -> 8.78 us  [broadcast_by_parts(): lax.all_to_all(jnp.stack([own] * lax.axis_size(axis)), axis, 0, 0)]
    all_to_all x0 -> x1, waiting for transfers between devices: none -> 5.53 us  [broadcast_by_parts(): lax.all_to_all(jnp.stack([own] * lax.axis_size(axis)), axis, 0, 0)]
  transfers between devices with their start and end apart: 2 -> 2, of which waited for: 2 -> 2; matrix products, arithmetic and copies ran while one was open for 10% -> 12% of each run, Pallas kernels for 0% -> 0%
where the time goes in v1:
time: 195 us; the launch traced here: 194 us
  waiting for transfers between devices  124 us (64%)
  local copies, waits for them, and re-layouts  22.8 us (12%)
  between operations  14.3 us (7%)
  blocking collectives  13.1 us (7%)
  starting transfers between devices  8.78 us (5%)
  matrix products  7.78 us (4%)
  other arithmetic  3.49 us (2%)
    reduce_scatter x1, waiting for transfers between devices, broadcast_by_parts(): own = lax.psum_scatter(padded, axis, scatter_dimension=0, tiled=True)  118 us
    all_to_all x1, blocking collectives, sum_at_owner(): lax.all_to_all(cut_along(value, dim, length), axis, 0, 0, tiled=True)  13.1 us
    dot_general x1, local copies, waits for them, and re-layouts, shards(): partial_out = jnp.dot(attn, w_out, preferred_element_type=jnp.float32)  12 us
    all_to_all x1, starting transfers between devices, broadcast_by_parts(): lax.all_to_all(jnp.stack([own] * lax.axis_size(axis)), axis, 0, 0)  8.78 us
    dot_general x1, matrix products, shards(): partial_out = jnp.dot(attn, w_out, preferred_element_type=jnp.float32)  5.64 us
    all_to_all x1, waiting for transfers between devices, broadcast_by_parts(): lax.all_to_all(jnp.stack([own] * lax.axis_size(axis)), axis, 0, 0)  5.53 us
    gather x2, local copies, waits for them, and re-layouts, shards(): cache_kv[:, pages].reshape(2, rows, maxpages * PAGE, groups_here, HD)  5.39 us
  transfers between devices with their start and end apart: 2, of which 2 were waited for; matrix products, arithmetic and copies ran while one was open for 12% of the time, Pallas kernels for 0%

profile of v1, /device:TPU:1, one launch (start us, length us, event | category | flops | bytes accessed | tf_op | source)
XLA Modules:
  0.0 193.9 jit_solution(17274023574642356115)
XLA Ops:
  6.5 0.0 copy-start
  6.5 0.0 reduce-scatter.2.cloned.1.call-start
  7.3 1.1 broadcast_select_fusion
  8.4 0.0 reduce-scatter.2.cloned.1.call-update
  8.4 118.2 %reduce-scatter.2.cloned.1.call-done = bf16[128,128]{1,0:T(8,128)(2,1)} async-done(((bf16[4096,128]{1,0:T(8,128)(2,1)}), bf16[128,128]{1,0:T(8,128)(2,1)}) %reduce-scatter.2.cloned.1.call-update) | async-done | bytes 32784 | tf_op jit(solution)/shard_map/reduce_scatter | solution.py:23
  126.6 2.0 %stack.2 = bf16[32,128,128]{2,1,0:T(8,128)(2,1)} broadcast(bf16[128,128]{1,0:T(8,128)(2,1)} %reduce-scatter.2.cloned.1.call-done), dimensions={1,2} | broadcast | bytes 1081344 | tf_op jit(solution)/shard_map/stack | solution.py:25
  128.6 8.8 %all-to-all-start = ((bf16[32,128,128]{2,1,0:T(8,128)(2,1)}), bf16[32,128,128]{2,1,0:T(8,128)(2,1)S(1)}, u32[]{:S(2)}, u32[]{:S(2)}) async-start(bf16[32,128,128]{2,1,0:T(8,128)(2,1)} %stack.2), calls=%async_computation.1 | async-start | bytes 2097152 | tf_op jit(solution)/shard_map/all_to_all | solution.py:25
  137.4 0.5 broadcast.57
  137.9 0.0 copy-done.4
  137.9 0.7 reduce.9
  138.5 0.1 reshape_squeeze.3
  138.6 0.1 reshape.148
  138.7 0.0 copy-done
  138.7 2.2 %gather_fusion = bf16[64,2,64,128]{3,2,1,0:T(8,128)(2,1)} fusion(bf16[2,64,64,128]{3,2,1,0:T(8,128)(2,1)S(1)} %copy-done, s32[1024]{0:T(1024)S(1)} %pad_clamp_fusion), kind=kCustom, calls=%fused_computation | custom fusion | bytes 4194560 | tf_op jit(solution)/shard_map/gather | solution.py:53
  140.9 3.2 %copy.23 = bf16[8,8,2,64,128]{4,3,1,0,2:T(8,128)(2,1)} copy(bf16[8,8,2,64,128]{4,3,2,1,0:T(8,128)(2,1)} %bitcast.54) | data formatting | bytes 4194304 | tf_op jit(solution)/shard_map/gather | solution.py:53
  144.1 12.0 %copy.13 = bf16[4096,1024]{1,0:T(8,128)(2,1)} copy(bf16[4096,1024]{0,1:T(8,128)(2,1)} %bitcast.55) | data formatting | bytes 16777216 | tf_op jit(solution)/shard_map/dot_general | solution.py:85
  156.1 0.0 copy-done.5
  156.1 0.6 compare_reduce_fusion
  156.7 0.1 iota_compare_fusion
  156.8 2.7 %fusion.18 = (bf16[1,8,8,64,128]{4,3,2,1,0:T(8,128)(2,1)S(1)}, bf16[1,8,8,64,128]{4,3,2,1,0:T(8,128)(2,1)}) fusion(bf16[2,8,8,64,128]{4,3,2,1,0:T(8,128)(2,1)} %bitcast.56), kind=kLoop, calls=%fused_computation.30 | loop fusion | bytes 4194304 | tf_op jit(solution)/shard_map/slice | solution.py:55
  159.5 0.0 copy-done.2
  159.5 0.5 fusion.20
  160.0 5.5 %all-to-all-done = bf16[32,128,128]{2,1,0:T(8,128)(2,1)S(1)} async-done(((bf16[32,128,128]{2,1,0:T(8,128)(2,1)}), bf16[32,128,128]{2,1,0:T(8,128)(2,1)S(1)}, u32[]{:S(2)}, u32[]{:S(2)}) %all-to-all-start) | async-done | bytes 1048608 | tf_op jit(solution)/shard_map/all_to_all | solution.py:25
  165.5 0.1 fusion.19
  165.6 1.1 fusion.21
  166.7 0.2 fusion.12
  166.9 0.3 convolution_bitcast_fusion.2
  167.2 0.2 fusion.7
  167.4 0.3 fusion.6
  167.8 5.6 %convolution_bitcast_fusion = f32[8,8,512]{2,1,0:T(8,128)S(1)} fusion(bf16[8,1024,1]{1,0,2:T(8,128)(2,1)S(1)} %reshape.157, bf16[8,512,1024]{2,1,0:T(8,128)(2,1)} %bitcast.53), kind=kOutput, calls=%fused_computation.5 | convolution fusion | flops 67108864 | bytes 8536064 | tf_op jit(solution)/shard_map/dot_general | solution.py:85
  173.4 13.1 %all_to_all.10 = f32[8,8,512]{2,1,0:T(8,128)S(1)} all-to-all(f32[8,8,512]{2,1,0:T(8,128)S(1)} %convolution_bitcast_fusion), channel_id=1, replica_groups=mesh['dp'=32,'tp'=8] {'tp'}, dimensions={0} | all-to-all | bytes 262144 | tf_op jit(solution)/shard_map/all_to_all | solution.py:37
  186.5 0.6 reduce_sum.29
  (12 shorter events, 0.1 us)
Async XLA Ops:
  6.5 132.2 %copy-start = (bf16[2,64,64,128]{3,2,1,0:T(8,128)(2,1)S(1)}, bf16[2,64,64,128]{3,2,1,0:T(8,128)(2,1)}, u32[]{:S(2)}) copy-start(bf16[2,64,64,128]{3,2,1,0:T(8,128)(2,1)} %param.10) | copy-start | bytes 6291460
  6.5 120.1 %reduce-scatter.2.cloned.1.call-start = ((), (), s32[]{:S(2)}) async-start(), calls=%async_computation.3 | async-start | bytes 1081344 | tf_op jit(solution)/shard_map/reduce_scatter | solution.py:23
  8.4 129.5 %copy-start.4 = (s32[1,64]{1,0:T(1,128)S(1)}, s32[1,64]{1,0:T(1,128)}, u32[]{:S(2)}) copy-start(s32[1,64]{1,0:T(1,128)} %param.12) | copy-start | bytes 772
  128.6 36.9 %all-to-all-start = ((bf16[32,128,128]{2,1,0:T(8,128)(2,1)}), bf16[32,128,128]{2,1,0:T(8,128)(2,1)S(1)}, u32[]{:S(2)}, u32[]{:S(2)}) async-start(bf16[32,128,128]{2,1,0:T(8,128)(2,1)} %stack.2), calls=%async_computation.1 | async-start | bytes 2097152 | tf_op jit(solution)/shard_map/all_to_all | solution.py:25
  144.1 12.0 %copy-start.5 = (s32[16]{0:T(128)S(1)}, s32[16]{0:T(128)}, u32[]{:S(2)}) copy-start(s32[16]{0:T(128)} %param.14) | copy-start | bytes 196
  144.1 12.6 %copy-start.3 = (s32[8]{0:T(128)S(1)}, s32[8]{0:T(128)}, u32[]{:S(2)}) copy-start(s32[8]{0:T(128)} %param.11) | copy-start | bytes 100
  156.8 2.7 %copy-start.2 = (bf16[8,1024]{1,0:T(8,128)(2,1)S(1)}, bf16[8,1024]{1,0:T(8,128)(2,1)}, u32[]{:S(2)}) copy-start(bf16[8,1024]{1,0:T(8,128)(2,1)} %param.8) | copy-start | bytes 49156
  165.5 1.4 copy-start.1
Sparse Core Ops, SparseCore 0:
  9.9 116.7 reduce-scatter.1
